TPU v7x, 32 devices: a whole 2x2x4 slice. The times are simulated.
32 devices in a mesh: band: 4 (over z), lev: 4 (over y, core), grp: 2 (over x).
Axes of the slice: x: 2, y: 2, z: 4, core: 2. Of those that a mesh axis runs over, the one named last changes fastest.
Arguments:
- fourier: bfloat16 [3, 8, 2, 2, 2, 48, 96], P(None, 'lev', None, None, 'grp', 'band'), may hold values from -6 to 6
- legendre: bfloat16 [96, 2, 48, 2, 48], P('band', None, 'lev', 'grp'), may hold values from -0.625 to 0.625
- lat_points: int32 [2, 48], P('grp', 'band'), may hold values from 20 to 400, as said below
- wave_slots: int32 [96], replicated, may hold values from 0 to 95, as said below
- vertical: float32 [8, 8], replicated, may hold values from -2 to 2
Outputs:
- spectral: bfloat16 [96, 2, 4, 8, 2, 48], P('band', None, None, None, None, ('lev', 'grp'))
Inputs may be any that keep to these rules, and one draw needn't show every extreme that they name: `lat_points`: the values are 20 + 4 i for i = 0 .. 95, each once (octahedral point counts of the latitude pairs, spread over devices). `wave_slots`: every wavenumber appears once; slots 2 i and 2 i + 1 hold wavenumbers m and 95 - m.
All inputs are finite; a program needn't handle non-finite values.
Results may differ from a plain program's by a relative error of at most 0.0053.
Values may be sent and summed in bfloat16 or wider, within the bound.
No kernel may reach another device: no remote copies, remote signals or barrier semaphores. Data moves between devices by JAX's collectives and lax.ppermute only.
A program may use at most 64 MiB of HBM per device.

v0:
```python
import jax
import jax.numpy as jnp
from jax import lax
from jax.sharding import PartitionSpec as P


def body(fourier, legendre, lat_points, wave_slots, vertical):
    wave_count = fourier.shape[6]
    cutoff = jnp.minimum(wave_count - 1, (lat_points - 1) // 2)
    wave_ids = lax.broadcasted_iota(jnp.int32, (1, 1, wave_count), 2)
    kept_mask = wave_ids <= cutoff[:, :, None]
    masked = jnp.where(kept_mask, fourier, jnp.zeros((), fourier.dtype))
    slot_table = (
        wave_slots[:, None] == lax.broadcasted_iota(jnp.int32, (wave_count, wave_count), 1)
    ).astype(jnp.bfloat16)
    ordered = lax.dot_general(
        slot_table, masked, (((1,), (6,)), ((), ())), preferred_element_type=jnp.float32
    ).astype(jnp.bfloat16)
    at_owners = lax.all_to_all(ordered, "band", split_axis=0, concat_axis=6, tiled=True)
    coeffs = lax.all_gather(at_owners, "lev", axis=2, tiled=True)
    level_count = coeffs.shape[2]
    level_rows = lax.broadcasted_iota(jnp.int32, (level_count, level_count), 0)
    level_cols = lax.broadcasted_iota(jnp.int32, (level_count, level_count), 1)
    integral = jnp.where(level_cols >= level_rows, vertical, jnp.zeros((), vertical.dtype))
    geopotential = jnp.einsum(
        "lk,skchgr->slchgr",
        integral,
        coeffs[:, 2].astype(jnp.float32),
        precision=lax.Precision.HIGHEST,
    ).astype(jnp.bfloat16)
    fields = jnp.concatenate([coeffs, geopotential[:, None]], axis=1)
    northern = fields[:, :, :, :, 0].astype(jnp.float32)
    southern = fields[:, :, :, :, 1].astype(jnp.float32)
    parity = jnp.stack(
        [(northern + southern).astype(jnp.bfloat16), (northern - southern).astype(jnp.bfloat16)],
        axis=4,
    )
    partial_value = lax.dot_general(
        parity, legendre, (((5, 6), (3, 4)), ((0, 4), (0, 1))), preferred_element_type=jnp.float32
    )
    summed = lax.psum_scatter(partial_value, "grp", scatter_dimension=5, tiled=True)
    slot_count = summed.shape[0]
    half_count = summed.shape[5]
    slot_waves = lax.dynamic_slice_in_dim(
        wave_slots, lax.axis_index("band") * slot_count, slot_count
    )
    block_start = (
        lax.axis_index("lev") * lax.axis_size("grp") + lax.axis_index("grp")
    ) * half_count
    half_ids = block_start + lax.broadcasted_iota(jnp.int32, (1, 1, half_count), 2)
    parity_ids = lax.broadcasted_iota(jnp.int32, (1, 2, 1), 1)
    total = slot_waves[:, None, None] + 2 * half_ids + parity_ids
    valid = (total <= wave_count - 1)[:, :, None, None, None, :]
    return jnp.where(valid, summed, 0.0).astype(jnp.bfloat16)


def solution(mesh):
    placed = (
        P(None, "lev", None, None, "grp", "band", None),
        P("band", None, "lev", "grp", None),
        P("grp", "band"),
        P(),
        P(),
    )
    return jax.shard_map(
        body,
        mesh=mesh,
        in_specs=placed,
        out_specs=P("band", None, None, None, None, ("lev", "grp")),
        check_vma=False,
    )
```

profile of v0, /device:TPU:0, one launch (start us, length us, event | category | flops | bytes accessed | tf_op | source)
XLA Modules:
  0.0 61.3 jit_solution(10844568631659761171)
XLA Ops:
  6.5 0.0 copy-start
  6.5 0.0 copy-start.2
  6.5 0.7 %minimum_bitcast_fusion = s32[12]{0:T(128)S(1)} fusion(s32[1,12]{1,0:T(1,128)} %param.7), kind=kLoop, calls=%fused_computation.34 | loop fusion | flops 204 | bytes 96 | tf_op jit(solution)/shard_map/le | solution.py:11
  7.3 0.1 iota_compare_fusion.1
  7.3 1.0 %fusion.9 = bf16[3,2,2,2,12,96]{5,3,4,2,1,0:T(2,128)(2,1)S(1)} fusion(bf16[3,2,2,2,1,12,96]{6,3,5,4,2,1,0:T(2,128)(2,1)} %param.5, pred[12,96]{1,0:T(8,128)(4,1)S(1)} %iota_compare_fusion.1), kind=kLoop, calls=%fused_computation.19 | loop fusion | flops 27648 | bytes 111744 | tf_op jit(solution)/shard_map/reshape.5
  8.3 0.9 %fusion.1 = bf16[96,3,2,2,2,1,12]{0,6,4,3,2,1,5:T(8,128)(2,1)S(1)} fusion(bf16[3,2,2,2,12,96]{5,3,4,2,1,0:T(2,128)(2,1)S(1)} %fusion.9, s32[96]{0:T(128)} %param.8), kind=kOutput, calls=%fused_computation.3 | convolution fusion | flops 5345280 | bytes 110976 | tf_op jit(solution)/shard_map/dot_general | solution.py:16
  9.2 0.7 %copy.19 = bf16[96,3,2,2,2,1,12]{6,4,3,2,1,5,0:T(2,128)(2,1)S(1)} copy(bf16[96,3,2,2,2,1,12]{0,6,4,3,2,1,5:T(8,128)(2,1)S(1)} %fusion.1) | data formatting | bytes 110592 | tf_op jit(solution)/shard_map/convert_element_type | solution.py:18
  9.8 1.7 %reshape.95 = bf16[4,2,3456]{2,1,0:T(2,128)(2,1)} reshape(bf16[96,1,3,2,2,2,12]{6,5,4,3,2,1,0:T(2,128)(2,1)S(1)} %bitcast.37) | data formatting | bytes 110592
  11.5 6.3 %all-to-all-start = ((bf16[4,2,3456]{2,1,0:T(2,128)(2,1)}), bf16[4,2,3456]{2,1,0:T(2,128)(2,1)S(1)}, u32[]{:S(2)}, u32[]{:S(2)}) async-start(bf16[4,2,3456]{2,1,0:T(2,128)(2,1)} %reshape.95), calls=%async_computation | async-start | bytes 110592 | tf_op jit(solution)/shard_map/all_to_all | solution.py:19
  17.9 0.0 reduce-scatter.2.cloned.1.call-start
  17.9 0.0 copy-done.2
  17.9 0.1 dynamic_slice.3
  17.9 5.6 %all-to-all-done = bf16[4,2,3456]{2,1,0:T(2,128)(2,1)S(1)} async-done(((bf16[4,2,3456]{2,1,0:T(2,128)(2,1)}), bf16[4,2,3456]{2,1,0:T(2,128)(2,1)S(1)}, u32[]{:S(2)}, u32[]{:S(2)}) %all-to-all-start) | async-done | bytes 55328 | tf_op jit(solution)/shard_map/all_to_all | solution.py:19
  23.6 1.4 %reshape.96 = bf16[96,1,3,2,2,2,12]{6,5,4,3,2,1,0:T(2,128)(2,1)S(1)} reshape(bf16[4,2,3456]{2,1,0:T(2,128)(2,1)S(1)} %all-to-all-done) | data formatting | bytes 110592
  25.0 1.0 %copy.32 = bf16[4,24,3,2,2,2,1,12]{1,0,5,7,4,3,2,6:T(4,128)(2,1)S(1)} copy(bf16[4,24,3,2,2,2,1,12]{7,5,4,3,2,1,0,6:T(2,128)(2,1)S(1)} %bitcast.38) | data formatting | bytes 110592 | tf_op jit(solution)/shard_map/all_to_all | solution.py:19
  26.0 0.0 copy-start.1
  26.0 0.2 copy.21
  26.2 0.2 copy.22
  26.4 7.6 %all_gather.3 = bf16[24,3,8,2,2,1,48]{6,0,5,4,3,1,2:T(8,128)(2,1)S(1)} all-gather(bf16[24,3,2,2,2,1,48]{6,0,5,4,3,1,2:T(8,128)(2,1)S(1)} %copy.22), channel_id=1, replica_groups=mesh['band'=4,'lev'=4,'grp'=2] {'lev'}, dimensions={2}, use_global_device_ids=true | all-gather | bytes 276480 | tf_op jit(solution)/shard_map/all_gather | solution.py:20
  34.0 0.2 copy_dynamic-update-slice_fusion
  34.2 0.0 copy-done.1
  34.2 0.3 fusion
  34.6 0.2 fusion.2
  34.8 0.0 copy-done
  34.8 0.4 fusion.4
  35.2 2.1 %copy.27 = f32[24,2,4,8,2,12]{0,3,4,2,1,5:T(8,128)} copy(f32[24,2,4,8,2,12]{5,3,4,2,1,0:T(8,128)S(1)} %fusion.4) | data formatting | bytes 294912 | tf_op jit(solution)/shard_map/dot_general | solution.py:38
  37.3 0.0 reduce-scatter.2.cloned.1.call-update
  37.3 0.1 broadcast_add_fusion
  37.4 15.2 %reduce-scatter.2.cloned.1.call-done = f32[24,2,4,8,2,6]{0,3,4,2,1,5:T(8,128)} async-done(((f32[24,2,4,8,2,12]{0,3,4,2,1,5:T(8,128)}), f32[24,2,4,8,2,6]{0,3,4,2,1,5:T(8,128)}) %reduce-scatter.2.cloned.1.call-update) | async-done | bytes 73744 | tf_op jit(solution)/shard_map/reduce_scatter | solution.py:41
  52.6 1.0 %select_convert_fusion = bf16[24,2,4,8,2,6]{0,3,4,2,1,5:T(8,128)(2,1)S(1)} fusion(f32[24,2,4,8,2,6]{0,3,4,2,1,5:T(8,128)} %reduce-scatter.2.cloned.1.call-done, pred[24,2,6]{0,1,2:T(4,128)(4,1)S(1)} %add_compare_fusion), kind=kLoop, calls=%fused_computation.13 | loop fusion | flops 18432 | bytes 110880 | tf_op jit(solution)/shard_map/convert_element_type | solution.py:54
  53.6 0.8 %copy.28 = bf16[24,2,4,8,2,6]{0,4,5,3,2,1:T(2,128)(2,1)} copy(bf16[24,2,4,8,2,6]{0,3,4,2,1,5:T(8,128)(2,1)S(1)} %select_convert_fusion) | data formatting | bytes 73728 | tf_op jit(solution)/shard_map/convert_element_type | solution.py:54
  (4 shorter events, 0.1 us)
Async XLA Ops:
  6.5 28.3 %copy-start = (bf16[24,2,12,1,48]{4,1,3,2,0:T(2,128)(2,1)S(1)}, bf16[24,2,12,1,48]{4,1,3,2,0:T(2,128)(2,1)}, u32[]{:S(2)}) copy-start(bf16[24,2,12,1,48]{4,1,3,2,0:T(2,128)(2,1)} %param.6) | copy-start | bytes 165892
  6.5 11.3 %copy-start.2 = (s32[96]{0:T(128)S(1)}, s32[96]{0:T(128)}, u32[]{:S(2)}) copy-start(s32[96]{0:T(128)} %param.8) | copy-start | bytes 1156
  11.5 12.1 %all-to-all-start = ((bf16[4,2,3456]{2,1,0:T(2,128)(2,1)}), bf16[4,2,3456]{2,1,0:T(2,128)(2,1)S(1)}, u32[]{:S(2)}, u32[]{:S(2)}) async-start(bf16[4,2,3456]{2,1,0:T(2,128)(2,1)} %reshape.95), calls=%async_computation | async-start | bytes 110592 | tf_op jit(solution)/shard_map/all_to_all | solution.py:19
  17.9 34.7 %reduce-scatter.2.cloned.1.call-start = ((), (), s32[]{:S(2)}) async-start(), calls=%async_computation.2 | async-start | bytes 1179648 | tf_op jit(solution)/shard_map/reduce_scatter | solution.py:41
  26.0 8.2 %copy-start.1 = (f32[8,8]{1,0:T(8,128)S(1)}, f32[8,8]{1,0:T(8,128)}, u32[]{:S(2)}) copy-start(f32[8,8]{1,0:T(8,128)} %param.9) | copy-start | bytes 772
Sparse Core Ops, SparseCore 0:
  37.4 15.1 reduce-scatter.1
where the time goes:
time: 61.6 us; the launch traced here: 61.3 us
  waiting for transfers between devices  20.9 us (34%)
  between operations  13.5 us (22%)
  local copies, waits for them, and re-layouts  8.37 us (14%)
  blocking collectives  7.56 us (12%)
  starting transfers between devices  6.35 us (10%)
  other arithmetic  3.09 us (5%)
  matrix products  1.56 us (3%)
    reduce_scatter x1, waiting for transfers between devices, body(): lax.psum_scatter(partial_value, 'grp', scatter_dimension=5, tiled=True)  15.2 us
    all_gather x1, blocking collectives, body(): coeffs = lax.all_gather(at_owners, 'lev', axis=2, tiled=True)  7.56 us
    all_to_all x1, starting transfers between devices, body(): lax.all_to_all(ordered, 'band', split_axis=0, concat_axis=6, tiled=True)  6.35 us
    all_to_all x1, waiting for transfers between devices, body(): lax.all_to_all(ordered, 'band', split_axis=0, concat_axis=6, tiled=True)  5.63 us
    unnamed x9, local copies, waits for them, and re-layouts  3.28 us
    dot_general x1, local copies, waits for them, and re-layouts, body(): lax.dot_general(parity, legendre, (((5, 6), (3, 4)), ((0, 4), (0, 1))), p...  2.07 us
    all_to_all x3, local copies, waits for them, and re-layouts, body(): lax.all_to_all(ordered, 'band', split_axis=0, concat_axis=6, tiled=True)  1.41 us
  transfers between devices with their start and end apart: 2, of which 2 were waited for; matrix products, arithmetic and copies ran while one was open for 0% of the time, Pallas kernels for 0%

commit v1 on v0

--- a/solution.py
+++ b/solution.py
@@ -17,7 +17,14 @@
         slot_table, masked, (((1,), (6,)), ((), ())), preferred_element_type=jnp.float32
     ).astype(jnp.bfloat16)
     at_owners = lax.all_to_all(ordered, "band", split_axis=0, concat_axis=6, tiled=True)
-    coeffs = lax.all_gather(at_owners, "lev", axis=2, tiled=True)
+    ways = lax.axis_size("lev")
+    pieces = [at_owners]
+    for far in range(1, ways):
+        pieces.append(
+            lax.ppermute(pieces[far - 1], "lev", [(d, (d - 1) % ways) for d in range(ways)])
+        )
+    line = jnp.concatenate(pieces, axis=2)
+    coeffs = jnp.roll(line, lax.axis_index("lev") * at_owners.shape[2], axis=2)
     level_count = coeffs.shape[2]
     level_rows = lax.broadcasted_iota(jnp.int32, (level_count, level_count), 0)
     level_cols = lax.broadcasted_iota(jnp.int32, (level_count, level_count), 1)

time: 61.6 us -> 69.1 us (1.12)
  blocking collectives: 7.56 us -> 11.9 us
  waiting for transfers between devices: 20.9 us -> 24.5 us
  starting transfers between devices: 6.35 us -> 3.84 us
  local copies, waits for them, and re-layouts: 8.37 us -> 10.5 us
    all_to_all x0 -> x1, blocking collectives: none -> 11.9 us  [body(): lax.all_to_all(ordered, 'band', split_axis=0, concat_axis=6, tiled=True)]
    ppermute x0 -> x3, waiting for transfers between devices: none -> 7.94 us  [body(): lax.ppermute(pieces[far - 1], 'lev', [(d, (d - 1) % ways) for d in range(...]
    all_gather x1 -> x0, blocking collectives: 7.56 us -> none  [body(): coeffs = lax.all_gather(at_owners, 'lev', axis=2, tiled=True)]
    all_to_all x1 -> x0, starting transfers between devices: 6.35 us -> none  [body(): lax.all_to_all(ordered, 'band', split_axis=0, concat_axis=6, tiled=True)]
    all_to_all x1 -> x0, waiting for transfers between devices: 5.63 us -> none  [body(): lax.all_to_all(ordered, 'band', split_axis=0, concat_axis=6, tiled=True)]
    ppermute x0 -> x3, starting transfers between devices: none -> 3.84 us  [body(): lax.ppermute(pieces[far - 1], 'lev', [(d, (d - 1) % ways) for d in range(...]
    concatenate x1, local copies, waits for them, and re-layouts: 0.04 us -> 2.14 us  [body(): coeffs = jnp.roll(line, lax.axis_index('lev') * at_owners.shape[2], axis=2)]
    reduce_scatter x1, waiting for transfers between devices: 15.2 us -> 16.6 us  [body(): lax.psum_scatter(partial_value, 'grp', scatter_dimension=5, tiled=True)]
  transfers between devices with their start and end apart: 2 -> 4, of which waited for: 2 -> 4; matrix products, arithmetic and copies ran while one was open for 0% -> 0% of each run, Pallas kernels for 0% -> 0%
where the time goes in v1:
time: 69.1 us; the launch traced here: 68.8 us
  waiting for transfers between devices  24.5 us (35%)
  between operations  13.5 us (20%)
  blocking collectives  11.9 us (17%)
  local copies, waits for them, and re-layouts  10.5 us (15%)
  starting transfers between devices  3.84 us (6%)
  other arithmetic  3.06 us (4%)
  matrix products  1.56 us (2%)
    reduce_scatter x1, waiting for transfers between devices, body(): lax.psum_scatter(partial_value, 'grp', scatter_dimension=5, tiled=True)  16.6 us
    all_to_all x1, blocking collectives, body(): lax.all_to_all(ordered, 'band', split_axis=0, concat_axis=6, tiled=True)  11.9 us
    ppermute x3, waiting for transfers between devices, body(): lax.ppermute(pieces[far - 1], 'lev', [(d, (d - 1) % ways) for d in range(...  7.94 us
    ppermute x3, starting transfers between devices, body(): lax.ppermute(pieces[far - 1], 'lev', [(d, (d - 1) % ways) for d in range(...  3.84 us
    unnamed x8, local copies, waits for them, and re-layouts  2.9 us
    concatenate x1, local copies, waits for them, and re-layouts, body(): coeffs = jnp.roll(line, lax.axis_index('lev') * at_owners.shape[2], axis=2)  2.14 us
    dot_general x1, local copies, waits for them, and re-layouts, body(): lax.dot_general(parity, legendre, (((5, 6), (3, 4)), ((0, 4), (0, 1))), p...  2.06 us
    all_to_all x3, local copies, waits for them, and re-layouts, body(): lax.all_to_all(ordered, 'band', split_axis=0, concat_axis=6, tiled=True)  1.61 us
  transfers between devices with their start and end apart: 4, of which 4 were waited for; matrix products, arithmetic and copies ran while one was open for 0% of the time, Pallas kernels for 0%

profile of v1, /device:TPU:0, one launch (start us, length us, event | category | flops | bytes accessed | tf_op | source)
XLA Modules:
  0.0 68.8 jit_solution(11029262747874184629)
XLA Ops:
  6.5 0.7 %minimum_bitcast_fusion = s32[12]{0:T(128)S(1)} fusion(s32[1,12]{1,0:T(1,128)} %param.7), kind=kLoop, calls=%fused_computation.35 | loop fusion | flops 204 | bytes 96 | tf_op jit(solution)/shard_map/le | solution.py:11
  7.2 0.1 iota_compare_fusion.1
  7.3 1.0 %fusion.9 = bf16[3,2,2,2,12,96]{5,3,4,2,1,0:T(2,128)(2,1)S(1)} fusion(bf16[3,2,2,2,1,12,96]{6,3,5,4,2,1,0:T(2,128)(2,1)} %param.5, pred[12,96]{1,0:T(8,128)(4,1)S(1)} %iota_compare_fusion.1), kind=kLoop, calls=%fused_computation.20 | loop fusion | flops 27648 | bytes 111744 | tf_op jit(solution)/shard_map/reshape.5
  8.3 0.9 %fusion.1 = bf16[96,3,2,2,2,1,12]{0,6,4,3,2,1,5:T(8,128)(2,1)S(1)} fusion(bf16[3,2,2,2,12,96]{5,3,4,2,1,0:T(2,128)(2,1)S(1)} %fusion.9, s32[96]{0:T(128)} %param.8), kind=kOutput, calls=%fused_computation.3 | convolution fusion | flops 5345280 | bytes 110976 | tf_op jit(solution)/shard_map/dot_general | solution.py:16
  9.2 0.7 copy.21
  9.8 1.0 %reshape.95 = bf16[4,2,3456]{2,1,0:T(2,128)(2,1)S(1)} reshape(bf16[96,1,3,2,2,2,12]{6,5,4,3,2,1,0:T(2,128)(2,1)S(1)} %bitcast.38) | data formatting | bytes 110592
  10.9 11.9 %all_to_all.18 = bf16[4,2,3456]{2,1,0:T(2,128)(2,1)S(1)} all-to-all(bf16[4,2,3456]{2,1,0:T(2,128)(2,1)S(1)} %reshape.95), channel_id=1, replica_groups=mesh['band'=4,'lev'=4,'grp'=2] {'band'}, dimensions={0} | all-to-all | bytes 110592 | tf_op jit(solution)/shard_map/all_to_all | solution.py:19
  22.8 1.4 %reshape.96 = bf16[96,1,3,2,2,2,12]{6,5,4,3,2,1,0:T(2,128)(2,1)S(1)} reshape(bf16[4,2,3456]{2,1,0:T(2,128)(2,1)S(1)} %all_to_all.18) | data formatting | bytes 110592
  24.1 1.0 %copy.34 = bf16[4,24,3,2,2,2,1,12]{1,0,5,7,4,3,2,6:T(4,128)(2,1)S(1)} copy(bf16[4,24,3,2,2,2,1,12]{7,5,4,3,2,1,0,6:T(2,128)(2,1)S(1)} %bitcast.39) | data formatting | bytes 110592 | tf_op jit(solution)/shard_map/all_to_all | solution.py:19
  25.2 0.2 copy.23
  25.4 0.4 copy.25
  25.8 0.1 collective-permute-start
  25.8 2.7 %collective-permute-done = bf16[24,3,2,2,2,1,48]{6,2,4,3,0,5,1:T(2,128)(2,1)S(1)} collective-permute-done((bf16[24,3,2,2,2,1,48]{6,2,4,3,0,5,1:T(2,128)(2,1)S(1)}, bf16[24,3,2,2,2,1,48]{6,2,4,3,0,5,1:T(2,128)(2,1)S(1)}, u32[]{:S(2)}, u32[]{:S(2)}) %collective-permute-start) | collective-permute-done | bytes 55328 | tf_op jit(solution)/shard_map/ppermute | solution.py:24
  28.5 1.9 %collective-permute-start.1 = (bf16[24,3,2,2,2,1,48]{6,2,4,3,0,5,1:T(2,128)(2,1)S(1)}, bf16[24,3,2,2,2,1,48]{6,2,4,3,0,5,1:T(2,128)(2,1)S(1)}, u32[]{:S(2)}, u32[]{:S(2)}) collective-permute-start(bf16[24,3,2,2,2,1,48]{6,2,4,3,0,5,1:T(2,128)(2,1)S(1)} %collective-permute-done), channel_id=1, source_target_pairs={{0,6},{2,0},{4,2},{6,4},{1,7},{3,1},{5,3},{7,5},{8,14},{10,8},{12,... | collective-permute-start | bytes 165896 | tf_op jit(solution)/shard_map/ppermute | solution.py:24
  30.4 2.7 %collective-permute-done.1 = bf16[24,3,2,2,2,1,48]{6,2,4,3,0,5,1:T(2,128)(2,1)S(1)} collective-permute-done((bf16[24,3,2,2,2,1,48]{6,2,4,3,0,5,1:T(2,128)(2,1)S(1)}, bf16[24,3,2,2,2,1,48]{6,2,4,3,0,5,1:T(2,128)(2,1)S(1)}, u32[]{:S(2)}, u32[]{:S(2)}) %collective-permute-start.1) | collective-permute-done | bytes 55328 | tf_op jit(solution)/shard_map/ppermute | solution.py:24
  33.1 1.9 %collective-permute-start.2 = (bf16[24,3,2,2,2,1,48]{6,2,4,3,0,5,1:T(2,128)(2,1)S(1)}, bf16[24,3,2,2,2,1,48]{6,2,4,3,0,5,1:T(2,128)(2,1)S(1)}, u32[]{:S(2)}, u32[]{:S(2)}) collective-permute-start(bf16[24,3,2,2,2,1,48]{6,2,4,3,0,5,1:T(2,128)(2,1)S(1)} %collective-permute-done.1), channel_id=1, source_target_pairs={{0,6},{2,0},{4,2},{6,4},{1,7},{3,1},{5,3},{7,5},{8,14},{10,8},{12,... | collective-permute-start | bytes 165896 | tf_op jit(solution)/shard_map/ppermute | solution.py:24
  35.0 0.1 dynamic_slice.7
  35.0 2.6 %collective-permute-done.2 = bf16[24,3,2,2,2,1,48]{6,2,4,3,0,5,1:T(2,128)(2,1)S(1)} collective-permute-done((bf16[24,3,2,2,2,1,48]{6,2,4,3,0,5,1:T(2,128)(2,1)S(1)}, bf16[24,3,2,2,2,1,48]{6,2,4,3,0,5,1:T(2,128)(2,1)S(1)}, u32[]{:S(2)}, u32[]{:S(2)}) %collective-permute-start.2) | collective-permute-done | bytes 55328 | tf_op jit(solution)/shard_map/ppermute | solution.py:24
  37.6 2.1 %concatenate.9 = bf16[24,3,16,2,2,1,48]{6,2,4,3,0,5,1:T(8,128)(2,1)S(1)} concatenate(bf16[24,3,2,2,2,1,48]{6,2,4,3,0,5,1:T(2,128)(2,1)S(1)} %copy.25, bf16[24,3,2,2,2,1,48]{6,2,4,3,0,5,1:T(2,128)(2,1)S(1)} %collective-permute-done, bf16[24,3,2,2,2,1,48]{6,2,4,3,0,5,1:T(2,128)(2,1)S(1)} %collective-permute-done.1, bf16[24,3,2,2,2,1,48]{6,2,4,3,0,5,1:T(2,128)(2,1)S(1)} %collective-permute-done.2, ...), dimensions={2} | concatenate | bytes 884736 | tf_op jit(solution)/shard_map/jit(_roll_dynamic)/concatenate | solution.py:27
  39.8 0.0 copy-start.1
  39.8 0.2 constant_dynamic-slice_fusion
  40.0 0.5 copy-done.1
  40.5 0.3 fusion
  40.8 0.2 fusion.2
  41.0 0.0 copy-done
  41.0 0.4 fusion.4
  41.4 2.1 %copy.29 = f32[24,2,4,8,2,12]{0,3,4,2,1,5:T(8,128)} copy(f32[24,2,4,8,2,12]{5,3,4,2,1,0:T(8,128)S(1)} %fusion.4) | data formatting | bytes 294912 | tf_op jit(solution)/shard_map/dot_general | solution.py:45
  43.4 0.0 reduce-scatter.2.cloned.1.call-update
  43.5 0.1 broadcast_add_fusion
  43.5 16.6 %reduce-scatter.2.cloned.1.call-done = f32[24,2,4,8,2,6]{0,3,4,2,1,5:T(8,128)} async-done(((f32[24,2,4,8,2,12]{0,3,4,2,1,5:T(8,128)}), f32[24,2,4,8,2,6]{0,3,4,2,1,5:T(8,128)}) %reduce-scatter.2.cloned.1.call-update) | async-done | bytes 73744 | tf_op jit(solution)/shard_map/reduce_scatter | solution.py:48
  60.1 1.0 %select_convert_fusion = bf16[24,2,4,8,2,6]{0,3,4,2,1,5:T(8,128)(2,1)S(1)} fusion(f32[24,2,4,8,2,6]{0,3,4,2,1,5:T(8,128)} %reduce-scatter.2.cloned.1.call-done, pred[24,2,6]{0,1,2:T(4,128)(4,1)S(1)} %add_compare_fusion), kind=kLoop, calls=%fused_computation.15 | loop fusion | flops 18432 | bytes 110880 | tf_op jit(solution)/shard_map/convert_element_type | solution.py:61
  61.2 0.8 %copy.30 = bf16[24,2,4,8,2,6]{0,4,5,3,2,1:T(2,128)(2,1)} copy(bf16[24,2,4,8,2,6]{0,3,4,2,1,5:T(8,128)(2,1)S(1)} %select_convert_fusion) | data formatting | bytes 73728 | tf_op jit(solution)/shard_map/convert_element_type | solution.py:61
  (6 shorter events, 0.0 us)
Async XLA Ops:
  6.5 34.5 %copy-start = (bf16[24,2,12,1,48]{4,1,3,2,0:T(2,128)(2,1)S(1)}, bf16[24,2,12,1,48]{4,1,3,2,0:T(2,128)(2,1)}, u32[]{:S(2)}) copy-start(bf16[24,2,12,1,48]{4,1,3,2,0:T(2,128)(2,1)} %param.6) | copy-start | bytes 165892
  6.5 53.6 %reduce-scatter.2.cloned.1.call-start = ((), (), s32[]{:S(2)}) async-start(), calls=%async_computation.2 | async-start | bytes 1179648 | tf_op jit(solution)/shard_map/reduce_scatter | solution.py:48
  22.7 12.2 %copy-start.2 = (s32[96]{0:T(128)S(1)}, s32[96]{0:T(128)}, u32[]{:S(2)}) copy-start(s32[96]{0:T(128)} %param.8) | copy-start | bytes 1156
  25.8 2.7 %collective-permute-start = (bf16[24,3,2,2,2,1,48]{6,2,4,3,0,5,1:T(2,128)(2,1)S(1)}, bf16[24,3,2,2,2,1,48]{6,2,4,3,0,5,1:T(2,128)(2,1)S(1)}, u32[]{:S(2)}, u32[]{:S(2)}) collective-permute-start(bf16[24,3,2,2,2,1,48]{6,2,4,3,0,5,1:T(2,128)(2,1)S(1)} %copy.25), channel_id=1, source_target_pairs={{0,6},{2,0},{4,2},{6,4},{1,7},{3,1},{5,3},{7,5},{8,14},{10,8},{12,... | collective-permute-start | bytes 165896 | tf_op jit(solution)/shard_map/ppermute | solution.py:24
  28.5 4.6 %collective-permute-start.1 = (bf16[24,3,2,2,2,1,48]{6,2,4,3,0,5,1:T(2,128)(2,1)S(1)}, bf16[24,3,2,2,2,1,48]{6,2,4,3,0,5,1:T(2,128)(2,1)S(1)}, u32[]{:S(2)}, u32[]{:S(2)}) collective-permute-start(bf16[24,3,2,2,2,1,48]{6,2,4,3,0,5,1:T(2,128)(2,1)S(1)} %collective-permute-done), channel_id=1, source_target_pairs={{0,6},{2,0},{4,2},{6,4},{1,7},{3,1},{5,3},{7,5},{8,14},{10,8},{12,... | collective-permute-start | bytes 165896 | tf_op jit(solution)/shard_map/ppermute | solution.py:24
  33.1 4.6 %collective-permute-start.2 = (bf16[24,3,2,2,2,1,48]{6,2,4,3,0,5,1:T(2,128)(2,1)S(1)}, bf16[24,3,2,2,2,1,48]{6,2,4,3,0,5,1:T(2,128)(2,1)S(1)}, u32[]{:S(2)}, u32[]{:S(2)}) collective-permute-start(bf16[24,3,2,2,2,1,48]{6,2,4,3,0,5,1:T(2,128)(2,1)S(1)} %collective-permute-done.1), channel_id=1, source_target_pairs={{0,6},{2,0},{4,2},{6,4},{1,7},{3,1},{5,3},{7,5},{8,14},{10,8},{12,... | collective-permute-start | bytes 165896 | tf_op jit(solution)/shard_map/ppermute | solution.py:24
  39.8 0.7 %copy-start.1 = (f32[8,8]{1,0:T(8,128)S(1)}, f32[8,8]{1,0:T(8,128)}, u32[]{:S(2)}) copy-start(f32[8,8]{1,0:T(8,128)} %param.9) | copy-start | bytes 772
Sparse Core Ops, SparseCore 0:
  43.6 16.4 reduce-scatter.1
